TPU v7x, 32 devices: a whole 2x2x4 slice. The times are simulated.
32 devices in a mesh: src: 4 (over z), dst: 8 (over y, x, core).
Axes of the slice: x: 2, y: 2, z: 4, core: 2. Of those that a mesh axis runs over, the one named last changes fastest.
Arguments:
- table: float32 [65536, 400], P(('src', 'dst')), may hold values from -2 to 2
- state: float32 [65536], P(('src', 'dst')), may hold values from 0.0001 to 0.01
- relations: float32 [4096, 400], replicated, may hold values from -4 to 4
- rel_ids: int32 [65536], P(('src', 'dst')), may hold values from 0 to 4095
- block_list: int32 [32, 32], P(('src', 'dst')), may hold values from 0 to 15
- src_pos: int32 [65536], P(('src', 'dst')), may hold values from 0 to 4095, as said below
- dst_pos: int32 [65536], P(('src', 'dst')), may hold values from 0 to 4095, as said below
- neg_pos: int32 [4096], P(('src', 'dst')), may hold values from 0 to 4095, as said below
Outputs:
- new_table: float32 [65536, 400], P(('src', 'dst'))
- new_state: float32 [65536], P(('src', 'dst'))
Inputs may be any that keep to these rules, and one draw needn't show every extreme that they name: Each entry is owner * 128 + row of a block the device requested; one device's src_pos, dst_pos and neg_pos name the same 16 owners, and its src_pos names each of them. `dst_pos`: rows of the same 16 owners as the device's src_pos. `neg_pos`: rows of the same 16 owners as the device's src_pos.
All inputs are finite; a program needn't handle non-finite values.
Results may differ from a plain program's by a relative error of at most 0.0004.
The roundings to bfloat16 on the way count: a program that leaves them out, or rounds other values in their place, can miss the bound.
Values may be sent and summed in bfloat16 or wider, within the bound.
No kernel may reach another device: no remote copies, remote signals or barrier semaphores. Data moves between devices by JAX's collectives and lax.ppermute only.
A program may use at most 192 MiB of HBM per device.

v0:
```python
import jax
import jax.numpy as jnp
from jax import lax
from jax.sharding import PartitionSpec as P

BLK = 128


def per_device(table, state, relations, rel_ids, block_list, src_pos, dst_pos, neg_pos):
    devices = lax.axis_size(("src", "dst"))
    rows_dev, width = table.shape
    blocks = rows_dev // BLK
    wanted = lax.all_to_all(
        block_list.reshape(devices, 1), ("src", "dst"), split_axis=0, concat_axis=0, tiled=True
    )
    asked = wanted.reshape(devices)
    outgoing = table.reshape(blocks, BLK, width).astype(jnp.bfloat16)[asked]
    fetched = lax.all_to_all(outgoing, ("src", "dst"), split_axis=0, concat_axis=0, tiled=True)
    flat = fetched.reshape(devices * BLK, width)
    source = flat[src_pos].astype(jnp.float32)
    target = flat[dst_pos].astype(jnp.float32)
    own_negs = flat[neg_pos]
    negs = lax.all_gather(own_negs, "dst", axis=0, tiled=True)
    operator = relations[rel_ids]
    u_full = source * operator
    u_half = u_full.astype(jnp.bfloat16)
    positive = jnp.sum(u_full * target, axis=1)
    scores = jnp.dot(u_half, negs.T, preferred_element_type=jnp.float32)
    g_pos = -jax.nn.sigmoid(-positive)
    g_neg = (jax.nn.sigmoid(scores) / negs.shape[0]).astype(jnp.bfloat16)
    grad_u = g_pos[:, None] * target + jnp.dot(g_neg, negs, preferred_element_type=jnp.float32)
    grad_src = grad_u * operator
    grad_dst = g_pos[:, None] * u_full
    own_neg_grad = lax.psum_scatter(
        jnp.dot(g_neg.T, u_half, preferred_element_type=jnp.float32).astype(jnp.bfloat16),
        "dst",
        scatter_dimension=0,
        tiled=True,
    ).astype(jnp.float32)
    slots = jnp.zeros((devices * BLK, width), jnp.float32)
    slots = slots.at[src_pos].add(grad_src).at[dst_pos].add(grad_dst).at[neg_pos].add(own_neg_grad)
    returned = lax.all_to_all(
        slots.reshape(devices, BLK, width), ("src", "dst"), split_axis=0, concat_axis=0, tiled=True
    )
    selector = (asked[None, :] == jnp.arange(blocks, dtype=jnp.int32)[:, None]).astype(jnp.float32)
    grad = jnp.einsum("bq,qrw->brw", selector, returned, precision=lax.Precision.HIGHEST).reshape(
        rows_dev, width
    )
    new_state = state + jnp.mean(grad * grad, axis=1)
    new_table = table - 0.1 * grad / (jnp.sqrt(new_state)[:, None] + 1e-10)
    return (new_table, new_state)


def solution(mesh):
    in_specs = (
        P(("src", "dst"), None),
        P(("src", "dst")),
        P(),
        P(("src", "dst")),
        P(("src", "dst"), None),
        P(("src", "dst")),
        P(("src", "dst")),
        P(("src", "dst")),
    )
    out_specs = (P(("src", "dst"), None), P(("src", "dst")))
    return jax.shard_map(
        per_device, mesh=mesh, in_specs=in_specs, out_specs=out_specs, check_vma=False
    )
```

profile of v0, /device:TPU:0, one launch (start us, length us, event | category | flops | bytes accessed | tf_op | source)
XLA Modules:
  0.0 411.0 jit_solution(8003938198328237329)
XLA Ops:
  7.2 1.3 copy.54
  8.5 7.3 %all-to-all-start = ((s32[32,1,1]{2,1,0:T(1,128)}), s32[32,1,1]{2,1,0:T(1,128)S(1)}, u32[]{:S(2)}, u32[]{:S(2)}) async-start(s32[32,1,1]{2,1,0:T(1,128)} %copy.54), calls=%async_computation | async-start | bytes 32768 | tf_op jit(solution)/shard_map/all_to_all | solution.py:13
  15.8 2.1 copy_bitcast_fusion
  18.0 4.9 %all-to-all-done = s32[32,1,1]{2,1,0:T(1,128)S(1)} async-done(((s32[32,1,1]{2,1,0:T(1,128)}), s32[32,1,1]{2,1,0:T(1,128)S(1)}, u32[]{:S(2)}, u32[]{:S(2)}) %all-to-all-start) | async-done | bytes 160 | tf_op jit(solution)/shard_map/all_to_all | solution.py:13
  22.9 0.7 reduce.1
  23.6 2.7 gather_fusion
  26.2 3.5 all-to-all-start.1
  29.8 0.0 copy-start.6
  29.8 0.0 reduce-scatter.4.cloned.1.call-start
  29.8 8.5 %copy.59 = f32[4096,400]{1,0:T(8,128)} copy(f32[4096,400]{0,1:T(8,128)} %param.10) | data formatting | bytes 13107200 | tf_op args[2]
  38.4 0.0 copy-done.6
  38.4 12.9 %gather_fusion.2 = f32[2048,400]{1,0:T(8,128)} fusion(f32[4096,400]{1,0:T(8,128)} %copy.59, s32[2048]{0:T(1024)S(1)} %fusion.9), kind=kCustom, calls=%fused_computation.2 | custom fusion | bytes 6561792 | tf_op jit(solution)/shard_map/gather | solution.py:24
  51.3 0.0 copy-start.8
  51.3 0.0 copy-start.4
  51.3 0.0 copy-start.5
  51.3 3.8 copy.60
  55.1 0.0 copy-done.8
  55.1 0.0 copy-done.4
  55.2 0.0 copy-done.5
  55.2 48.9 %all-to-all-done.1 = bf16[32,128,400]{1,2,0:T(8,128)(2,1)} async-done(((bf16[32,128,400]{1,2,0:T(8,128)(2,1)}), bf16[32,128,400]{1,2,0:T(8,128)(2,1)}, u32[]{:S(2)}, u32[]{:S(2)}) %all-to-all-start.1) | async-done | bytes 3276832 | tf_op jit(solution)/shard_map/all_to_all | solution.py:18
  104.1 6.0 %copy.72 = bf16[32,128,400]{2,1,0:T(8,128)(2,1)} copy(bf16[32,128,400]{1,2,0:T(8,128)(2,1)} %all-to-all-done.1) | data formatting | bytes 6553600 | tf_op jit(solution)/shard_map/reshape | solution.py:19
  110.1 3.6 gather_fusion.4
  113.7 11.9 %all-gather = bf16[1024,400]{1,0:T(8,128)(2,1)} all-gather(bf16[128,400]{1,0:T(8,128)(2,1)S(1)} %gather_fusion.4), channel_id=2, replica_groups=mesh['src'=4,'dst'=8] {'dst'}, dimensions={0}, use_global_device_ids=true | all-gather | bytes 921600 | tf_op jit(solution)/shard_map/all_gather | solution.py:23
  125.6 12.0 %gather_fusion.3 = bf16[2048,400]{1,0:T(8,128)(2,1)} fusion(bf16[4096,400]{1,0:T(8,128)(2,1)} %bitcast.33, s32[2048]{0:T(1024)S(1)} %get-tuple-element.7), kind=kCustom, calls=%fused_computation.3 | custom fusion | bytes 3284992 | tf_op jit(solution)/shard_map/gather | solution.py:21
  137.6 12.0 %gather_fusion.1 = bf16[2048,400]{1,0:T(8,128)(2,1)} fusion(bf16[4096,400]{1,0:T(8,128)(2,1)} %bitcast.34, s32[2048]{0:T(1024)S(1)} %get-tuple-element.8), kind=kCustom, calls=%fused_computation.1 | custom fusion | bytes 3284992 | tf_op jit(solution)/shard_map/gather | solution.py:20
  149.5 3.9 copy.58
  153.4 3.8 copy.62
  157.2 0.0 copy-start
  157.2 0.0 copy-start.3
  157.3 2.8 fusion.4
  160.0 0.0 copy-done
  160.0 0.0 copy-done.3
  160.0 4.1 %multiply_convert_fusion = bf16[2048,1024]{1,0:T(8,128)(2,1)S(1)} fusion(bf16[1024,400]{1,0:T(8,128)(2,1)S(1)} %copy-done.3, f32[2048,400]{0,1:T(8,128)S(1)} %copy.60, bf16[2048,400]{0,1:T(8,128)(2,1)S(1)} %copy-done), kind=kOutput, calls=%fused_computation.8 | convolution fusion | flops 1690664960 | bytes 9928704 | tf_op jit(solution)/shard_map/dot_general | solution.py:28
  164.2 0.0 copy-start.1
  164.2 1.9 copy-done.1
  166.1 2.9 convolution_convert_fusion
  169.0 2.2 copy.70
  171.2 0.0 reduce-scatter.4.cloned.1.call-update
  171.2 3.6 broadcast_multiply_fusion.1
  174.8 5.1 %copy.66 = f32[2048,400]{1,0:T(8,128)} copy(f32[2048,400]{0,1:T(8,128)} %broadcast_multiply_fusion.1) | data formatting | bytes 6553600 | tf_op jit(solution)/shard_map/mul | solution.py:33
  179.9 7.0 %fusion.6 = f32[2048,400]{0,1:T(8,128)} fusion(f32[2048,400]{0,1:T(8,128)S(1)} %copy.60, bf16[2048,400]{0,1:T(8,128)(2,1)} %copy.62, bf16[2048,1024]{1,0:T(8,128)(2,1)} %copy-done.1, bf16[1024,400]{1,0:T(8,128)(2,1)} %all-gather, f32[2048]{0:T(1024)S(1)} %divide_negate_fusion), kind=kOutput, calls=%fused_computation.17 | convolution fusion | flops 1680998400 | bytes 13213696 | tf_op jit(solution)/shard_map/dot_general | solution.py:31
  186.9 5.0 %copy.65 = f32[2048,400]{1,0:T(8,128)} copy(f32[2048,400]{0,1:T(8,128)} %fusion.6) | data formatting | bytes 6553600 | tf_op jit(solution)/shard_map/mul | solution.py:32
  191.9 17.2 %scatter_custom_fusion = f32[4096,400]{1,0:T(8,128)} fusion(s32[2048]{0:T(1024)S(1)} %get-tuple-element.9, f32[2048,400]{1,0:T(8,128)} %copy.65, f32[]{:T(128)} %constant.9.clone.1), kind=kCustom, calls=%fused_computation.11 | custom fusion | flops 819200 | bytes 6554112 | tf_op jit(solution)/shard_map/scatter-add | solution.py:41
  209.0 19.8 %scatter_fusion = f32[4096,400]{1,0:T(8,128)} fusion(f32[4096,400]{1,0:T(8,128)} %scatter_custom_fusion, s32[2048]{0:T(1024)S(1)} %get-tuple-element.6, f32[2048,400]{1,0:T(8,128)} %copy.66), kind=kCustom, calls=%fused_computation.6 | custom fusion | flops 819200 | bytes 9838592 | tf_op jit(solution)/shard_map/scatter-add | solution.py:41
  228.8 0.0 reduce-scatter.4.cloned.1.call-done
  228.8 1.0 copy.71
  229.8 0.1 copy.67
  229.9 7.9 %scatter_fusion.1 = f32[4096,400]{1,0:T(8,128)} fusion(f32[4096,400]{1,0:T(8,128)} %scatter_fusion, s32[128]{0:T(128)S(1)} %compare_select_fusion.3, f32[128,400]{1,0:T(8,128)S(1)} %copy.67), kind=kCustom, calls=%fused_computation.7 | custom fusion | flops 51200 | bytes 614912 | tf_op jit(solution)/shard_map/scatter-add | solution.py:41
  237.8 8.7 %copy.68 = f32[32,128,400]{1,2,0:T(8,128)} copy(f32[32,128,400]{2,1,0:T(8,128)} %bitcast.35) | data formatting | bytes 13107200 | tf_op jit(solution)/shard_map/reshape | solution.py:43
  246.5 149.1 %all_to_all.22 = f32[32,128,400]{1,2,0:T(8,128)S(1)} all-to-all(f32[32,128,400]{1,2,0:T(8,128)} %copy.68), channel_id=1, replica_groups=mesh['src'=4,'dst'=8] {'src','dst'}, dimensions={0} | all-to-all | bytes 13107200 | tf_op jit(solution)/shard_map/all_to_all | solution.py:42
  395.6 0.0 copy-start.7
  395.6 0.0 copy-start.2
  395.6 4.5 %multiply_reduce_fusion = (f32[16,128]{1,0:T(8,128)S(1)}, f32[16,128,400]{1,0,2:T(8,128)S(1)}) fusion(f32[32,128,400]{1,2,0:T(8,128)S(1)} %all_to_all.22, s32[32]{0:T(128)S(1)} %reduce.1), kind=kOutput, calls=%fused_computation.20 | convolution fusion | flops 317028864 | bytes 9838720 | tf_op jit(solution)/shard_map/bq,qrw->brw/dot_general | solution.py:46
  400.1 0.0 copy-done.7
  400.1 0.6 sqrt_add_fusion
  400.7 0.0 copy-done.2
  400.7 3.5 fusion.7
  (8 shorter events, 0.1 us)
Async XLA Ops:
  8.5 14.4 %all-to-all-start = ((s32[32,1,1]{2,1,0:T(1,128)}), s32[32,1,1]{2,1,0:T(1,128)S(1)}, u32[]{:S(2)}, u32[]{:S(2)}) async-start(s32[32,1,1]{2,1,0:T(1,128)} %copy.54), calls=%async_computation | async-start | bytes 32768 | tf_op jit(solution)/shard_map/all_to_all | solution.py:13
  26.2 77.8 %all-to-all-start.1 = ((bf16[32,128,400]{1,2,0:T(8,128)(2,1)}), bf16[32,128,400]{1,2,0:T(8,128)(2,1)}, u32[]{:S(2)}, u32[]{:S(2)}) async-start(bf16[32,128,400]{1,2,0:T(8,128)(2,1)} %gather_fusion), calls=%async_computation.1 | async-start | bytes 6553600 | tf_op jit(solution)/shard_map/all_to_all | solution.py:18
  29.8 8.6 %copy-start.6 = (s32[2048]{0:T(1024)S(1)}, s32[2048]{0:T(1024)}, u32[]{:S(2)}) copy-start(s32[2048]{0:T(1024)} %param.11) | copy-start | bytes 24580
  29.8 199.0 %reduce-scatter.4.cloned.1.call-start = ((), (), s32[]{:S(2)}) async-start(), calls=%async_computation.4 | async-start | bytes 1179648
  51.3 3.8 copy-start.8
  51.3 3.8 copy-start.4
  51.3 3.8 copy-start.5
  157.2 2.8 copy-start
  157.2 2.8 copy-start.3
  164.2 1.9 copy-start.1
  395.6 4.5 %copy-start.7 = (f32[2048]{0:T(1024)S(1)}, f32[2048]{0:T(1024)}, u32[]{:S(2)}) copy-start(f32[2048]{0:T(1024)} %param.9) | copy-start | bytes 24580
  395.6 5.1 %copy-start.2 = (f32[2048,400]{0,1:T(8,128)S(1)}, f32[2048,400]{0,1:T(8,128)}, u32[]{:S(2)}) copy-start(f32[2048,400]{0,1:T(8,128)} %param.8) | copy-start | bytes 9830404
Sparse Core Ops, SparseCore 0:
  171.4 34.9 reduce-scatter.3
where the time goes:
time: 412 us; the launch traced here: 411 us
  blocking collectives  161 us (39%)
  local copies, waits for them, and re-layouts  94.6 us (23%)
  other arithmetic  58.1 us (14%)
  waiting for transfers between devices  53.8 us (13%)
  matrix products  18.4 us (4%)
  between operations  14.2 us (3%)
  starting transfers between devices  10.9 us (3%)
    all_to_all x1, blocking collectives, per_device(): lax.all_to_all(slots.reshape(devices, BLK, width), ('src', 'dst'), split_...  149 us
    all_to_all x1, waiting for transfers between devices, per_device(): lax.all_to_all(outgoing, ('src', 'dst'), split_axis=0, concat_axis=0, til...  48.9 us
    scatter-add x3, other arithmetic, per_device(): slots.at[src_pos].add(grad_src).at[dst_pos].add(grad_dst).at[neg_pos]  44.8 us
    gather x2, local copies, waits for them, and re-layouts, per_device(): operator = relations[rel_ids]  16.7 us
    gather x2, local copies, waits for them, and re-layouts, per_device(): source = flat[src_pos].astype(jnp.float32)  15.8 us
    gather x2, local copies, waits for them, and re-layouts, per_device(): target = flat[dst_pos].astype(jnp.float32)  15.8 us
    unnamed x21, local copies, waits for them, and re-layouts  13.7 us
    all_gather x1, blocking collectives, per_device(): negs = lax.all_gather(own_negs, 'dst', axis=0, tiled=True)  11.9 us
  transfers between devices with their start and end apart: 3, of which 2 were waited for; matrix products, arithmetic and copies ran while one was open for 21% of the time, Pallas kernels for 0%

commit v1 on v0

--- a/solution.py
+++ b/solution.py
@@ -2,8 +2,41 @@
 import jax.numpy as jnp
 from jax import lax
 from jax.sharding import PartitionSpec as P
+from jax.lax import axis_index, ppermute, psum
 
 BLK = 128
+
+
+def touch_forms_over_axis(here_x, shard_axis):
+    everything, carry, local_part = (
+        psum(1, axis_name=shard_axis),
+        axis_index(shard_axis),
+        here_x.shape[0],
+    )
+    arrivals = tuple((kk * everything if ix == 0 else kk for ix, kk in enumerate(here_x.shape)))
+    row_out = lax.dynamic_update_slice_in_dim(
+        jnp.zeros(arrivals, here_x.dtype), here_x, carry * local_part, axis=0
+    )
+    even = arr_now = here_x
+    for to_i in range(1, everything // 2 + 1):
+        even = ppermute(
+            even,
+            axis_name=shard_axis,
+            perm=tuple(((ix, (ix + 1) % everything) for ix in range(everything))),
+        )
+        row_out = lax.dynamic_update_slice_in_dim(
+            row_out, even, (carry - to_i) % everything * local_part, axis=0
+        )
+        if 2 * to_i < everything:
+            arr_now = ppermute(
+                arr_now,
+                axis_name=shard_axis,
+                perm=tuple(((ix, (ix - 1) % everything) for ix in range(everything))),
+            )
+            row_out = lax.dynamic_update_slice_in_dim(
+                row_out, arr_now, (carry + to_i) % everything * local_part, axis=0
+            )
+    return row_out
 
 
 def per_device(table, state, relations, rel_ids, block_list, src_pos, dst_pos, neg_pos):
@@ -20,7 +53,7 @@
     source = flat[src_pos].astype(jnp.float32)
     target = flat[dst_pos].astype(jnp.float32)
     own_negs = flat[neg_pos]
-    negs = lax.all_gather(own_negs, "dst", axis=0, tiled=True)
+    negs = touch_forms_over_axis(own_negs, "dst")
     operator = relations[rel_ids]
     u_full = source * operator
     u_half = u_full.astype(jnp.bfloat16)

time: 412 us -> 422 us (1.024)
  blocking collectives: 161 us -> 149 us
  waiting for transfers between devices: 53.8 us -> 64.4 us
  starting transfers between devices: 10.9 us -> 18.9 us
    ppermute x0 -> x7, waiting for transfers between devices: none -> 12 us  [the longest x4 12 us: touch_forms_over_axis(): ppermute(even, axis_name=shard_axis, perm=tuple(((ix, (ix + 1) % everythi...]
    all_gather x1 -> x0, blocking collectives: 11.9 us -> none  [per_device(): negs = lax.all_gather(own_negs, 'dst', axis=0, tiled=True)]
    ppermute x0 -> x7, starting transfers between devices: none -> 8.02 us  [the longest x3 7.9 us: touch_forms_over_axis(): ppermute(arr_now, axis_name=shard_axis, perm=tuple(((ix, (ix - 1) % every...]
    unnamed x21 -> x29, local copies, waits for them, and re-layouts: 13.7 us -> 13.8 us
  transfers between devices with their start and end apart: 3 -> 10, of which waited for: 2 -> 5; matrix products, arithmetic and copies ran while one was open for 21% -> 29% of each run, Pallas kernels for 0% -> 0%
where the time goes in v1:
time: 422 us; the launch traced here: 420 us
  blocking collectives  149 us (35%)
  local copies, waits for them, and re-layouts  96.5 us (23%)
  waiting for transfers between devices  64.4 us (15%)
  other arithmetic  59 us (14%)
  starting transfers between devices  18.9 us (4%)
  matrix products  18.3 us (4%)
  between operations  14.5 us (3%)
    all_to_all x1, blocking collectives, per_device(): lax.all_to_all(slots.reshape(devices, BLK, width), ('src', 'dst'), split_...  149 us
    all_to_all x1, waiting for transfers between devices, per_device(): lax.all_to_all(outgoing, ('src', 'dst'), split_axis=0, concat_axis=0, til...  47.5 us
    scatter-add x3, other arithmetic, per_device(): slots.at[src_pos].add(grad_src).at[dst_pos].add(grad_dst).at[neg_pos]  44.6 us
    gather x2, local copies, waits for them, and re-layouts, per_device(): operator = relations[rel_ids]  16.7 us
    gather x2, local copies, waits for them, and re-layouts, per_device(): target = flat[dst_pos].astype(jnp.float32)  16.6 us
    gather x2, local copies, waits for them, and re-layouts, per_device(): source = flat[src_pos].astype(jnp.float32)  15.8 us
    unnamed x29, local copies, waits for them, and re-layouts  13.8 us
    ppermute x4, waiting for transfers between devices, touch_forms_over_axis(): ppermute(even, axis_name=shard_axis, perm=tuple(((ix, (ix + 1) % everythi...  12 us
  transfers between devices with their start and end apart: 10, of which 5 were waited for; matrix products, arithmetic and copies ran while one was open for 29% of the time, Pallas kernels for 0%

profile of v1, /device:TPU:0, one launch (start us, length us, event | category | flops | bytes accessed | tf_op | source)
XLA Modules:
  0.0 420.2 jit_solution(3993552249931156064)
XLA Ops:
  7.2 1.3 copy.54
  8.5 7.3 %all-to-all-start = ((s32[32,1,1]{2,1,0:T(1,128)}), s32[32,1,1]{2,1,0:T(1,128)S(1)}, u32[]{:S(2)}, u32[]{:S(2)}) async-start(s32[32,1,1]{2,1,0:T(1,128)} %copy.54), calls=%async_computation | async-start | bytes 32768 | tf_op jit(solution)/shard_map/all_to_all | solution.py:46
  15.8 2.1 copy_bitcast_fusion
  18.0 4.9 %all-to-all-done = s32[32,1,1]{2,1,0:T(1,128)S(1)} async-done(((s32[32,1,1]{2,1,0:T(1,128)}), s32[32,1,1]{2,1,0:T(1,128)S(1)}, u32[]{:S(2)}, u32[]{:S(2)}) %all-to-all-start) | async-done | bytes 160 | tf_op jit(solution)/shard_map/all_to_all | solution.py:46
  22.9 0.7 reduce.1
  23.6 2.7 gather_fusion
  26.3 0.0 copy-done.8
  26.3 3.5 all-to-all-start.1
  29.8 0.0 reduce-scatter.4.cloned.1.call-start
  30.0 0.0 copy-start.6
  30.0 8.5 %copy.59 = f32[4096,400]{1,0:T(8,128)} copy(f32[4096,400]{0,1:T(8,128)} %param.10) | data formatting | bytes 13107200 | tf_op args[2]
  38.5 0.0 copy-done.6
  38.5 13.0 %gather_fusion.2 = f32[2048,400]{1,0:T(8,128)} fusion(f32[4096,400]{1,0:T(8,128)} %copy.59, s32[2048]{0:T(1024)S(1)} %fusion.9), kind=kCustom, calls=%fused_computation.2 | custom fusion | bytes 6561792 | tf_op jit(solution)/shard_map/gather | solution.py:57
  51.5 3.8 copy.60
  55.3 0.0 copy-done.12
  55.4 0.0 copy-start.10
  55.4 0.0 copy-done.4
  55.4 0.6 broadcast_clamp_fusion.1
  56.0 0.0 copy-done.5
  56.0 0.6 compare_select_fusion
  56.6 47.5 %all-to-all-done.1 = bf16[32,128,400]{1,2,0:T(8,128)(2,1)} async-done(((bf16[32,128,400]{1,2,0:T(8,128)(2,1)}), bf16[32,128,400]{1,2,0:T(8,128)(2,1)}, u32[]{:S(2)}, u32[]{:S(2)}) %all-to-all-start.1) | async-done | bytes 3276832 | tf_op jit(solution)/shard_map/all_to_all | solution.py:51
  104.1 6.0 %copy.72 = bf16[32,128,400]{2,1,0:T(8,128)(2,1)} copy(bf16[32,128,400]{1,2,0:T(8,128)(2,1)} %all-to-all-done.1) | data formatting | bytes 6553600 | tf_op jit(solution)/shard_map/reshape | solution.py:52
  110.1 3.6 gather_fusion.4
  113.7 0.1 collective-permute-start
  113.7 2.6 collective-permute-start.1
  116.4 12.7 %gather_fusion.3 = bf16[2048,400]{1,0:T(8,128)(2,1)} fusion(bf16[4096,400]{1,0:T(8,128)(2,1)} %bitcast.33, s32[2048]{0:T(1024)} %get-tuple-element.7), kind=kCustom, calls=%fused_computation.3 | custom fusion | bytes 3284992 | tf_op jit(solution)/shard_map/gather | solution.py:54
  129.1 12.0 %gather_fusion.1 = bf16[2048,400]{1,0:T(8,128)(2,1)} fusion(bf16[4096,400]{1,0:T(8,128)(2,1)} %bitcast.34, s32[2048]{0:T(1024)S(1)} %get-tuple-element.8), kind=kCustom, calls=%fused_computation.1 | custom fusion | bytes 3284992 | tf_op jit(solution)/shard_map/gather | solution.py:53
  141.1 3.8 copy.58
  144.9 3.9 copy.62
  148.8 2.7 fusion.4
  151.5 0.1 broadcast_in_dim.30
  151.6 0.0 collective-permute-done
  151.7 0.1 collective-permute-start.2
  151.7 0.0 collective-permute-done.1
  151.7 2.6 collective-permute-start.3
  154.4 0.9 constant_dynamic-update-slice_fusion.6
  155.3 3.0 collective-permute-done.2
  158.3 0.0 collective-permute-start.4
  158.3 0.0 collective-permute-done.3
  158.3 2.6 collective-permute-start.5
  161.0 3.7 collective-permute-done.4
  164.7 0.0 collective-permute-start.6
  164.7 0.0 collective-permute-done.5
  164.8 5.2 %collective-permute-done.6 = bf16[128,400]{1,0:T(8,128)(2,1)S(1)} collective-permute-done((bf16[128,400]{1,0:T(8,128)(2,1)S(1)}, bf16[128,400]{1,0:T(8,128)(2,1)S(1)}, u32[]{:S(2)}, u32[]{:S(2)}) %collective-permute-start.6) | collective-permute-done | bytes 102432 | tf_op jit(solution)/shard_map/ppermute | solution.py:22
  170.0 4.1 multiply_convert_fusion
  174.2 1.9 copy-done.1
  176.1 2.9 convolution_convert_fusion
  179.0 2.2 copy.70
  181.2 0.0 reduce-scatter.4.cloned.1.call-update
  181.2 3.6 broadcast_multiply_fusion.1
  184.8 5.1 %copy.66 = f32[2048,400]{1,0:T(8,128)} copy(f32[2048,400]{0,1:T(8,128)} %broadcast_multiply_fusion.1) | data formatting | bytes 6553600 | tf_op jit(solution)/shard_map/mul | solution.py:66
  189.9 6.9 %fusion.6 = f32[2048,400]{0,1:T(8,128)} fusion(f32[2048,400]{0,1:T(8,128)S(1)} %copy.60, bf16[2048,400]{0,1:T(8,128)(2,1)} %copy.62, bf16[2048,1024]{1,0:T(8,128)(2,1)} %copy-done.1, bf16[1024,400]{1,0:T(8,128)(2,1)} %copy-done.3, f32[2048]{0:T(1024)S(1)} %divide_negate_fusion), kind=kOutput, calls=%fused_computation.17 | convolution fusion | flops 1680998400 | bytes 13213696 | tf_op jit(solution)/shard_map/dot_general | solution.py:64
  196.8 5.0 %copy.65 = f32[2048,400]{1,0:T(8,128)} copy(f32[2048,400]{0,1:T(8,128)} %fusion.6) | data formatting | bytes 6553600 | tf_op jit(solution)/shard_map/mul | solution.py:65
  201.8 16.9 %scatter_custom_fusion = f32[4096,400]{1,0:T(8,128)} fusion(s32[2048]{0:T(1024)} %get-tuple-element.9, f32[2048,400]{1,0:T(8,128)} %copy.65, f32[]{:T(128)} %constant.65.clone.1), kind=kCustom, calls=%fused_computation.11 | custom fusion | flops 819200 | bytes 6554112 | tf_op jit(solution)/shard_map/scatter-add | solution.py:74
  218.7 19.8 %scatter_fusion = f32[4096,400]{1,0:T(8,128)} fusion(f32[4096,400]{1,0:T(8,128)} %scatter_custom_fusion, s32[2048]{0:T(1024)S(1)} %get-tuple-element.6, f32[2048,400]{1,0:T(8,128)} %copy.66), kind=kCustom, calls=%fused_computation.6 | custom fusion | flops 819200 | bytes 9838592 | tf_op jit(solution)/shard_map/scatter-add | solution.py:74
  238.5 1.0 copy.71
  239.5 0.1 copy.67
  239.7 7.9 %scatter_fusion.1 = f32[4096,400]{1,0:T(8,128)} fusion(f32[4096,400]{1,0:T(8,128)} %scatter_fusion, s32[128]{0:T(128)S(1)} %copy-done.11, f32[128,400]{1,0:T(8,128)S(1)} %copy.67), kind=kCustom, calls=%fused_computation.7 | custom fusion | flops 51200 | bytes 614912 | tf_op jit(solution)/shard_map/scatter-add | solution.py:74
  247.5 8.7 %copy.68 = f32[32,128,400]{1,2,0:T(8,128)} copy(f32[32,128,400]{2,1,0:T(8,128)} %bitcast.35) | data formatting | bytes 13107200 | tf_op jit(solution)/shard_map/reshape | solution.py:76
  256.2 148.5 %all_to_all.22 = f32[32,128,400]{1,2,0:T(8,128)S(1)} all-to-all(f32[32,128,400]{1,2,0:T(8,128)} %copy.68), channel_id=1, replica_groups=mesh['src'=4,'dst'=8] {'src','dst'}, dimensions={0} | all-to-all | bytes 13107200 | tf_op jit(solution)/shard_map/all_to_all | solution.py:75
  404.8 4.5 %multiply_reduce_fusion = (f32[16,128]{1,0:T(8,128)S(1)}, f32[16,128,400]{1,0,2:T(8,128)S(1)}) fusion(f32[32,128,400]{1,2,0:T(8,128)S(1)} %all_to_all.22, s32[32]{0:T(128)S(1)} %copy-done.9), kind=kOutput, calls=%fused_computation.20 | convolution fusion | flops 317028864 | bytes 9838720 | tf_op jit(solution)/shard_map/bq,qrw->brw/dot_general | solution.py:79
  409.3 0.0 copy-done.7
  409.3 0.6 sqrt_add_fusion
  409.9 3.5 fusion.7
  (31 shorter events, 0.2 us)
Async XLA Ops:
  8.5 14.4 %all-to-all-start = ((s32[32,1,1]{2,1,0:T(1,128)}), s32[32,1,1]{2,1,0:T(1,128)S(1)}, u32[]{:S(2)}, u32[]{:S(2)}) async-start(s32[32,1,1]{2,1,0:T(1,128)} %copy.54), calls=%async_computation | async-start | bytes 32768 | tf_op jit(solution)/shard_map/all_to_all | solution.py:46
  23.5 2.7 copy-start.8
  26.3 77.8 %all-to-all-start.1 = ((bf16[32,128,400]{1,2,0:T(8,128)(2,1)}), bf16[32,128,400]{1,2,0:T(8,128)(2,1)}, u32[]{:S(2)}, u32[]{:S(2)}) async-start(bf16[32,128,400]{1,2,0:T(8,128)(2,1)} %gather_fusion), calls=%async_computation.1 | async-start | bytes 6553600 | tf_op jit(solution)/shard_map/all_to_all | solution.py:51
  29.8 208.7 %reduce-scatter.4.cloned.1.call-start = ((), (), s32[]{:S(2)}) async-start(), calls=%async_computation.4 | async-start | bytes 1179648
  30.0 8.6 %copy-start.6 = (s32[2048]{0:T(1024)S(1)}, s32[2048]{0:T(1024)}, u32[]{:S(2)}) copy-start(s32[2048]{0:T(1024)} %param.11) | copy-start | bytes 24580
  51.5 3.8 copy-start.12
  51.5 3.9 copy-start.4
  51.5 4.5 %copy-start.5 = (s32[2048]{0:T(1024)S(1)}, s32[2048]{0:T(1024)}, u32[]{:S(2)}) copy-start(s32[2048]{0:T(1024)} %param.14) | copy-start | bytes 24580
  55.4 54.7 %copy-start.10 = (s32[128]{0:T(128)}, s32[128]{0:T(128)S(1)}, u32[]{:S(2)}) copy-start(s32[128]{0:T(128)S(1)} %compare_select_fusion.3) | copy-start | bytes 1540
  113.7 38.0 %collective-permute-start = (bf16[128,400]{1,0:T(8,128)(2,1)S(1)}, bf16[128,400]{1,0:T(8,128)(2,1)}, u32[]{:S(2)}, u32[]{:S(2)}) collective-permute-start(bf16[128,400]{1,0:T(8,128)(2,1)S(1)} %gather_fusion.4), channel_id=1, source_target_pairs={{0,1},{1,2},{2,3},{3,4},{4,5},{5,6},{6,7},{7,0},{8,9},{9,10},{10,1... | collective-permute-start | bytes 307208 | tf_op jit(solution)/shard_map/ppermute | solution.py:22
  113.7 38.0 %collective-permute-start.1 = (bf16[128,400]{1,0:T(8,128)(2,1)S(1)}, bf16[128,400]{1,0:T(8,128)(2,1)S(1)}, u32[]{:S(2)}, u32[]{:S(2)}) collective-permute-start(bf16[128,400]{1,0:T(8,128)(2,1)S(1)} %gather_fusion.4), channel_id=1, source_target_pairs={{0,7},{1,0},{2,1},{3,2},{4,3},{5,4},{6,5},{7,6},{8,15},{9,8},{10,9... | collective-permute-start | bytes 307208 | tf_op jit(solution)/shard_map/ppermute | solution.py:31
  148.8 21.2 %copy-start = (bf16[2048,400]{0,1:T(8,128)(2,1)S(1)}, bf16[2048,400]{0,1:T(8,128)(2,1)}, u32[]{:S(2)}) copy-start(bf16[2048,400]{0,1:T(8,128)(2,1)} %copy.58) | copy-start | bytes 4915204
  151.7 6.6 %collective-permute-start.2 = (bf16[128,400]{1,0:T(8,128)(2,1)}, bf16[128,400]{1,0:T(8,128)(2,1)S(1)}, u32[]{:S(2)}, u32[]{:S(2)}) collective-permute-start(bf16[128,400]{1,0:T(8,128)(2,1)} %collective-permute-done), channel_id=1, source_target_pairs={{0,1},{1,2},{2,3},{3,4},{4,5},{5,6},{6,7},{7,0},{8,9},{9,10},{10,1... | collective-permute-start | bytes 307208 | tf_op jit(solution)/shard_map/ppermute | solution.py:22
  151.7 6.6 %collective-permute-start.3 = (bf16[128,400]{1,0:T(8,128)(2,1)S(1)}, bf16[128,400]{1,0:T(8,128)(2,1)S(1)}, u32[]{:S(2)}, u32[]{:S(2)}) collective-permute-start(bf16[128,400]{1,0:T(8,128)(2,1)S(1)} %collective-permute-done.1), channel_id=1, source_target_pairs={{0,7},{1,0},{2,1},{3,2},{4,3},{5,4},{6,5},{7,6},{8,15},{9,8},{10,9... | collective-permute-start | bytes 307208 | tf_op jit(solution)/shard_map/ppermute | solution.py:31
  158.3 6.4 %collective-permute-start.4 = (bf16[128,400]{1,0:T(8,128)(2,1)S(1)}, bf16[128,400]{1,0:T(8,128)(2,1)S(1)}, u32[]{:S(2)}, u32[]{:S(2)}) collective-permute-start(bf16[128,400]{1,0:T(8,128)(2,1)S(1)} %collective-permute-done.2), channel_id=1, source_target_pairs={{0,1},{1,2},{2,3},{3,4},{4,5},{5,6},{6,7},{7,0},{8,9},{9,10},{10,1... | collective-permute-start | bytes 307208 | tf_op jit(solution)/shard_map/ppermute | solution.py:22
  158.3 6.4 %collective-permute-start.5 = (bf16[128,400]{1,0:T(8,128)(2,1)S(1)}, bf16[128,400]{1,0:T(8,128)(2,1)S(1)}, u32[]{:S(2)}, u32[]{:S(2)}) collective-permute-start(bf16[128,400]{1,0:T(8,128)(2,1)S(1)} %collective-permute-done.3), channel_id=1, source_target_pairs={{0,7},{1,0},{2,1},{3,2},{4,3},{5,4},{6,5},{7,6},{8,15},{9,8},{10,9... | collective-permute-start | bytes 307208 | tf_op jit(solution)/shard_map/ppermute | solution.py:31
  164.7 5.3 %collective-permute-start.6 = (bf16[128,400]{1,0:T(8,128)(2,1)S(1)}, bf16[128,400]{1,0:T(8,128)(2,1)S(1)}, u32[]{:S(2)}, u32[]{:S(2)}) collective-permute-start(bf16[128,400]{1,0:T(8,128)(2,1)S(1)} %collective-permute-done.4), channel_id=1, source_target_pairs={{0,1},{1,2},{2,3},{3,4},{4,5},{5,6},{6,7},{7,0},{8,9},{9,10},{10,1... | collective-permute-start | bytes 307208 | tf_op jit(solution)/shard_map/ppermute | solution.py:22
  170.0 4.1 copy-start.3
  174.2 1.9 copy-start.1
  218.7 20.9 %copy-start.11 = (s32[128]{0:T(128)S(1)}, s32[128]{0:T(128)}, u32[]{:S(2)}) copy-start(s32[128]{0:T(128)} %copy-done.10) | copy-start | bytes 1540
  256.2 148.5 %copy-start.9 = (s32[32]{0:T(128)S(1)}, s32[32]{0:T(128)}, u32[]{:S(2)}) copy-start(s32[32]{0:T(128)} %copy-done.8) | copy-start | bytes 388
  404.8 4.5 %copy-start.7 = (f32[2048]{0:T(1024)S(1)}, f32[2048]{0:T(1024)}, u32[]{:S(2)}) copy-start(f32[2048]{0:T(1024)} %param.9) | copy-start | bytes 24580
  404.8 5.1 %copy-start.2 = (f32[2048,400]{0,1:T(8,128)S(1)}, f32[2048,400]{0,1:T(8,128)}, u32[]{:S(2)}) copy-start(f32[2048,400]{0,1:T(8,128)} %param.8) | copy-start | bytes 9830404
Sparse Core Ops, SparseCore 0:
  181.3 33.7 reduce-scatter.3
